TPU v7x, 128 devices: a whole 4x4x4 slice. The times are simulated.
128 devices in a mesh: row: 16 (over y, x), col: 8 (over z, core).
Axes of the slice: x: 4, y: 4, z: 4, core: 2. Of those that a mesh axis runs over, the one named last changes fastest.
Arguments:
- owned_rows: bfloat16 [3072, 8192], P(('row', 'col')), may hold values from -6 to 6
- suffix_lengths: int32 [128], replicated, may hold values from 1 to 24, 1024 in all
- owner_map: int32 [128], replicated, may hold values from 0 to 127, each once
- prefix_lengths: int32 [128], replicated, may hold values from 0 to 4095
- gate_weight: bfloat16 [8192, 29568], P('row', 'col'), may hold values from -0.0625 to 0.0625
- up_weight: bfloat16 [8192, 29568], P('row', 'col'), may hold values from -0.0625 to 0.0625
- down_weight: bfloat16 [29568, 8192], P('col', 'row'), may hold values from -0.03125 to 0.03125
Outputs:
- mixed: bfloat16 [1024, 8192], P('col', 'row')
Inputs may be any that keep to these rules, and one draw needn't show every extreme that they name: `suffix_lengths`: the lengths add up to 1024; the largest is exactly 24. `owner_map`: each device owns one request; request r's suffix rows fill, in order, the first suffix_lengths[r] of the 24 slots of its owner in owned_rows, and the other slots are not used.
All inputs are finite; a program needn't handle non-finite values.
Results may differ from a plain program's by a relative error of at most 0.0049.
Values may be sent and summed in bfloat16 or wider, within the bound.
No kernel may reach another device: no remote copies, remote signals or barrier semaphores. Data moves between devices by JAX's collectives and lax.ppermute only.
A program may use at most 128 MiB of HBM per device.

v0:
```python
import jax
import jax.numpy as jnp
from jax import lax
from jax.sharding import PartitionSpec as P

TOK_DEV = 8


def source_rows(suffix_lengths, owner_map, prefix_lengths, row_count, slot_size):
    request_ids = jnp.arange(suffix_lengths.shape[0], dtype=jnp.int32)
    longer = prefix_lengths[None, :] > prefix_lengths[:, None]
    earlier = (prefix_lengths[None, :] == prefix_lengths[:, None]) & (
        request_ids[None, :] < request_ids[:, None]
    )
    starts = jnp.sum(jnp.where(longer | earlier, suffix_lengths[None, :], 0), axis=1)
    positions = jnp.arange(row_count, dtype=jnp.int32)
    ends = starts + suffix_lengths
    inside = (positions[:, None] >= starts[None, :]) & (positions[:, None] < ends[None, :])
    offsets = owner_map * slot_size - starts
    shifted = jnp.sum(jnp.where(inside, offsets[None, :], 0), axis=1)
    return positions + shifted


def on_device(
    owned_rows, suffix_lengths, owner_map, prefix_lengths, gate_weight, up_weight, down_weight
):
    slot_size = owned_rows.shape[0]
    total_rows = TOK_DEV * suffix_lengths.shape[0]
    source = source_rows(suffix_lengths, owner_map, prefix_lengths, total_rows, slot_size)
    gathered = lax.all_gather(owned_rows, "col", axis=0, tiled=True)
    feature_rows = lax.all_to_all(gathered, "row", split_axis=1, concat_axis=0, tiled=True)
    suffix_rows = jnp.take(feature_rows, source, axis=0)
    block_rows = suffix_rows
    gate_share = lax.psum_scatter(
        jnp.dot(block_rows, gate_weight, preferred_element_type=jnp.float32),
        "row",
        scatter_dimension=0,
        tiled=True,
    )
    block_rows = suffix_rows
    up_share = lax.psum_scatter(
        jnp.dot(block_rows, up_weight, preferred_element_type=jnp.float32),
        "row",
        scatter_dimension=0,
        tiled=True,
    )
    hidden_share = (jax.nn.silu(gate_share) * up_share).astype(jnp.bfloat16)
    partial_sums = jnp.dot(
        lax.all_gather(hidden_share, "row", axis=0, tiled=True),
        down_weight,
        preferred_element_type=jnp.float32,
    )
    return lax.psum_scatter(partial_sums, "col", scatter_dimension=0, tiled=True).astype(
        jnp.bfloat16
    )


def solution(mesh):
    return jax.shard_map(
        on_device,
        mesh=mesh,
        in_specs=(
            P(("row", "col"), None),
            P(),
            P(),
            P(),
            P("row", "col"),
            P("row", "col"),
            P("col", "row"),
        ),
        out_specs=P("col", "row"),
        check_vma=False,
    )
```

profile of v0, /device:TPU:0, one launch (start us, length us, event | category | flops | bytes accessed | tf_op | source)
XLA Modules:
  0.0 444.5 jit_solution(16864953255005129052)
XLA Ops:
  6.5 0.0 all-gather.3.cloned.1.call-start
  6.5 0.7 all-gather.3.cloned.1.call-update
  7.3 32.2 %all-gather.3.cloned.1.call-done = bf16[192,8192]{1,0:T(8,128)(2,1)} async-done(((bf16[24,8192]{1,0:T(8,128)(2,1)}), bf16[192,8192]{1,0:T(8,128)(2,1)}) %all-gather.3.cloned.1.call-update) | async-done | bytes 3145744 | tf_op jit(solution)/shard_map/all_gather | solution.py:30
  39.5 3.9 copy.13
  43.4 0.0 copy-start.1
  43.4 0.0 copy-start.2
  43.4 0.0 copy-start.3
  43.4 6.9 %all-to-all-start = ((bf16[192,16,512]{2,0,1:T(8,128)(2,1)}), bf16[192,16,512]{2,0,1:T(8,128)(2,1)S(1)}, u32[]{:S(2)}, u32[]{:S(2)}) async-start(bf16[192,16,512]{2,0,1:T(8,128)(2,1)} %bitcast.14), calls=%async_computation | async-start | bytes 6291456 | tf_op jit(solution)/shard_map/all_to_all | solution.py:31
  50.3 0.0 reduce-scatter.6.cloned.1.call-start
  50.4 0.0 copy-done.1
  50.4 0.0 copy-done.2
  50.4 0.2 select_reduce_fusion.1
  50.6 0.0 copy-done.3
  50.6 0.2 select_reduce_fusion
  50.8 48.1 %all-to-all-done = bf16[192,16,512]{2,0,1:T(8,128)(2,1)S(1)} async-done(((bf16[192,16,512]{2,0,1:T(8,128)(2,1)}), bf16[192,16,512]{2,0,1:T(8,128)(2,1)S(1)}, u32[]{:S(2)}, u32[]{:S(2)}) %all-to-all-start) | async-done | bytes 3145760 | tf_op jit(solution)/shard_map/all_to_all | solution.py:31
  98.9 5.0 %gather_fusion = bf16[1024,512]{1,0:T(8,128)(2,1)} fusion(bf16[3072,512]{1,0:T(8,128)(2,1)S(1)} %bitcast.13, s32[1024]{0:T(1024)S(1)} %broadcast_clamp_fusion), kind=kCustom, calls=%fused_computation | custom fusion | bytes 2101248 | tf_op jit(solution)/shard_map/jit(_take)/gather | solution.py:32
  104.0 12.0 %fusion.1 = f32[1024,3696]{1,0:T(8,128)} fusion(bf16[512,3696]{0,1:T(8,128)(2,1)} %param.12, bf16[1024,512]{1,0:T(8,128)(2,1)} %gather_fusion, pred[1024]{0:T(1024)(128)(4,1)S(1)} %compare_and_fusion), kind=kOutput, calls=%fused_computation.8 | convolution fusion | flops 3876061184 | bytes 19973120 | tf_op jit(solution)/shard_map/dot_general | solution.py:42
  116.0 0.0 copy-start
  116.0 0.0 reduce-scatter.6.cloned.1.call-update
  116.0 0.0 reduce-scatter.4.cloned.1.call-start
  116.1 1.1 copy-done
  117.2 10.0 %fusion.2 = f32[1024,3696]{1,0:T(8,128)} fusion(bf16[512,3696]{0,1:T(8,128)(2,1)} %param.11, bf16[1024,512]{1,0:T(8,128)(2,1)S(1)} %copy-done, pred[1024]{0:T(1024)(128)(4,1)S(1)} %compare_and_fusion), kind=kOutput, calls=%fused_computation.9 | convolution fusion | flops 3876061184 | bytes 19973120 | tf_op jit(solution)/shard_map/dot_general | solution.py:35
  127.2 0.0 reduce-scatter.4.cloned.1.call-update
  127.2 0.0 all-gather.5.cloned.1.call-start
  127.3 90.2 %reduce-scatter.6.cloned.1.call-done = f32[64,3696]{1,0:T(8,128)} async-done(((f32[1024,3696]{1,0:T(8,128)}), f32[64,3696]{1,0:T(8,128)}) %reduce-scatter.6.cloned.1.call-update) | async-done | bytes 946192 | tf_op jit(solution)/shard_map/reduce_scatter | solution.py:41
  217.5 106.2 %reduce-scatter.4.cloned.1.call-done = f32[64,3696]{1,0:T(8,128)} async-done(((f32[1024,3696]{1,0:T(8,128)}), f32[64,3696]{1,0:T(8,128)}) %reduce-scatter.4.cloned.1.call-update) | async-done | bytes 946192 | tf_op jit(solution)/shard_map/reduce_scatter | solution.py:34
  323.7 2.5 multiply_convert_fusion
  326.2 0.0 all-gather.5.cloned.1.call-update
  326.2 0.0 reduce-scatter.8.cloned.1.call-start
  326.3 66.2 %all-gather.5.cloned.1.call-done = bf16[1024,3696]{1,0:T(8,128)(2,1)} async-done(((bf16[64,3696]{1,0:T(8,128)(2,1)}), bf16[1024,3696]{1,0:T(8,128)(2,1)}) %all-gather.5.cloned.1.call-update) | async-done | bytes 7569424 | tf_op jit(solution)/shard_map/all_gather | solution.py:49
  392.5 9.8 %fusion.8 = f32[1024,512]{1,0:T(8,128)} fusion(bf16[1024,3696]{1,0:T(8,128)(2,1)} %all-gather.5.cloned.1.call-done, bf16[3696,512]{1,0:T(8,128)(2,1)} %param.13), kind=kOutput, calls=%fused_computation.22 | convolution fusion | flops 3875536896 | bytes 13451264 | tf_op jit(solution)/shard_map/dot_general | solution.py:48
  402.3 0.0 reduce-scatter.8.cloned.1.call-update
  402.3 34.0 %reduce-scatter.8.cloned.1.call-done = f32[128,512]{1,0:T(8,128)} async-done(((f32[1024,512]{1,0:T(8,128)}), f32[128,512]{1,0:T(8,128)}) %reduce-scatter.8.cloned.1.call-update) | async-done | bytes 262160 | tf_op jit(solution)/shard_map/reduce_scatter | solution.py:53
  436.3 1.6 convert_element_type.7
  (4 shorter events, 0.0 us)
Async XLA Ops:
  6.5 32.9 %all-gather.3.cloned.1.call-start = ((), (), s32[]{:S(2)}) async-start(), calls=%async_computation.4 | async-start | bytes 3538944 | tf_op jit(solution)/shard_map/all_gather | solution.py:30
  43.4 7.0 %copy-start.1 = (s32[128]{0:T(128)S(1)}, s32[128]{0:T(128)}, u32[]{:S(2)}) copy-start(s32[128]{0:T(128)} %param.10) | copy-start | bytes 1540
  43.4 7.0 %copy-start.2 = (s32[128]{0:T(128)S(1)}, s32[128]{0:T(128)}, u32[]{:S(2)}) copy-start(s32[128]{0:T(128)} %param.8) | copy-start | bytes 1540
  43.4 7.2 %copy-start.3 = (s32[128]{0:T(128)S(1)}, s32[128]{0:T(128)}, u32[]{:S(2)}) copy-start(s32[128]{0:T(128)} %param.9) | copy-start | bytes 1540
  43.4 55.6 %all-to-all-start = ((bf16[192,16,512]{2,0,1:T(8,128)(2,1)}), bf16[192,16,512]{2,0,1:T(8,128)(2,1)S(1)}, u32[]{:S(2)}, u32[]{:S(2)}) async-start(bf16[192,16,512]{2,0,1:T(8,128)(2,1)} %bitcast.14), calls=%async_computation | async-start | bytes 6291456 | tf_op jit(solution)/shard_map/all_to_all | solution.py:31
  50.3 167.1 %reduce-scatter.6.cloned.1.call-start = ((), (), s32[]{:S(2)}) async-start(), calls=%async_computation.6 | async-start | bytes 16154624 | tf_op jit(solution)/shard_map/reduce_scatter | solution.py:41
  116.0 1.2 copy-start
  116.0 207.6 %reduce-scatter.4.cloned.1.call-start = ((), (), s32[]{:S(2)}) async-start(), calls=%async_computation.5 | async-start | bytes 16154624 | tf_op jit(solution)/shard_map/reduce_scatter | solution.py:34
  127.2 265.2 %all-gather.5.cloned.1.call-start = ((), (), s32[]{:S(2)}) async-start(), calls=%async_computation.7 | async-start | bytes 8077312 | tf_op jit(solution)/shard_map/all_gather | solution.py:49
  326.2 110.1 %reduce-scatter.8.cloned.1.call-start = ((), (), s32[]{:S(2)}) async-start(), calls=%async_computation.8 | async-start | bytes 2359296 | tf_op jit(solution)/shard_map/reduce_scatter | solution.py:53
Sparse Core Ops, SparseCore 0:
  9.0 30.3 all-gather.2
  116.2 101.2 reduce-scatter.5
  220.9 102.7 reduce-scatter.3
  326.4 66.0 all-gather.4
  402.5 33.8 reduce-scatter.7
where the time goes:
time: 445 us; the launch traced here: 444 us
  waiting for transfers between devices  378 us (85%)
  matrix products  31.9 us (7%)
  between operations  13.2 us (3%)
  local copies, waits for them, and re-layouts  10.1 us (2%)
  starting transfers between devices  7.11 us (2%)
  other arithmetic  4.55 us (1%)
    reduce_scatter x1, waiting for transfers between devices, on_device(): lax.psum_scatter(jnp.dot(block_rows, gate_weight, preferred_element_type=...  106 us
    reduce_scatter x1, waiting for transfers between devices, on_device(): lax.psum_scatter(jnp.dot(block_rows, up_weight, preferred_element_type=jn...  90.2 us
    all_gather x1, waiting for transfers between devices, on_device(): lax.all_gather(hidden_share, 'row', axis=0, tiled=True)  66.2 us
    all_to_all x1, waiting for transfers between devices, on_device(): lax.all_to_all(gathered, 'row', split_axis=1, concat_axis=0, tiled=True)  48.1 us
    reduce_scatter x1, waiting for transfers between devices, on_device(): lax.psum_scatter(partial_sums, 'col', scatter_dimension=0, tiled=True)  34 us
    all_gather x1, waiting for transfers between devices, on_device(): gathered = lax.all_gather(owned_rows, 'col', axis=0, tiled=True)  32.2 us
    dot_general x1, matrix products, on_device(): jnp.dot(block_rows, up_weight, preferred_element_type=jnp.float32)  12 us
    dot_general x1, matrix products, on_device(): jnp.dot(block_rows, gate_weight, preferred_element_type=jnp.float32)  9.97 us
  transfers between devices with their start and end apart: 6, of which 6 were waited for; matrix products, arithmetic and copies ran while one was open for 2% of the time, Pallas kernels for 0%

commit v1 on v0

--- a/solution.py
+++ b/solution.py
@@ -4,6 +4,11 @@
 from jax.sharding import PartitionSpec as P
 
 TOK_DEV = 8
+
+
+def swapped_in(x, mesh_axis, dim):
+    sent = jnp.stack([x] * lax.axis_size(mesh_axis))
+    return jnp.concatenate(lax.all_to_all(sent, mesh_axis, 0, 0), axis=dim)
 
 
 def source_rows(suffix_lengths, owner_map, prefix_lengths, row_count, slot_size):
@@ -46,9 +51,7 @@
     )
     hidden_share = (jax.nn.silu(gate_share) * up_share).astype(jnp.bfloat16)
     partial_sums = jnp.dot(
-        lax.all_gather(hidden_share, "row", axis=0, tiled=True),
-        down_weight,
-        preferred_element_type=jnp.float32,
+        swapped_in(hidden_share, "row", 0), down_weight, preferred_element_type=jnp.float32
     )
     return lax.psum_scatter(partial_sums, "col", scatter_dimension=0, tiled=True).astype(
         jnp.bfloat16

time: 445 us -> 464 us (1.043)
  blocking collectives: 0 us -> 91.8 us
  waiting for transfers between devices: 378 us -> 309 us
    all_to_all x0 -> x1, blocking collectives: none -> 91.8 us  [swapped_in(): return jnp.concatenate(lax.all_to_all(sent, mesh_axis, 0, 0), axis=dim)]
    all_gather x1 -> x0, waiting for transfers between devices: 66.2 us -> none  [on_device(): lax.all_gather(hidden_share, 'row', axis=0, tiled=True)]
  transfers between devices with their start and end apart: 6 -> 5, of which waited for: 6 -> 5; matrix products, arithmetic and copies ran while one was open for 2% -> 2% of each run, Pallas kernels for 0% -> 0%
where the time goes in v1:
time: 464 us
  waiting for transfers between devices  309 us (67%)
  blocking collectives  91.8 us (20%)
  matrix products  27.6 us (6%)
  between operations  13.2 us (3%)
  local copies, waits for them, and re-layouts  10.9 us (2%)
  starting transfers between devices  7.07 us (2%)
    reduce_scatter x1, waiting for transfers between devices, on_device(): lax.psum_scatter(jnp.dot(block_rows, gate_weight, preferred_element_type=...  106 us
    all_to_all x1, blocking collectives, swapped_in(): return jnp.concatenate(lax.all_to_all(sent, mesh_axis, 0, 0), axis=dim)  91.8 us
    reduce_scatter x1, waiting for transfers between devices, on_device(): lax.psum_scatter(jnp.dot(block_rows, up_weight, preferred_element_type=jn...  90.2 us
    all_to_all x1, waiting for transfers between devices, on_device(): lax.all_to_all(gathered, 'row', split_axis=1, concat_axis=0, tiled=True)  48.1 us
    all_gather x1, waiting for transfers between devices, on_device(): gathered = lax.all_gather(owned_rows, 'col', axis=0, tiled=True)  32.2 us
    reduce_scatter x1, waiting for transfers between devices, on_device(): lax.psum_scatter(partial_sums, 'col', scatter_dimension=0, tiled=True)  31.7 us
    dot_general x1, matrix products, on_device(): jnp.dot(block_rows, up_weight, preferred_element_type=jnp.float32)  12 us
    dot_general x1, matrix products, on_device(): jnp.dot(block_rows, gate_weight, preferred_element_type=jnp.float32)  9.97 us
  transfers between devices with their start and end apart: 5, of which 5 were waited for; matrix products, arithmetic and copies ran while one was open for 2% of the time, Pallas kernels for 0%

profile of v1, /device:TPU:0, one launch (start us, length us, event | category | flops | bytes accessed | tf_op | source)
XLA Modules:
  0.0 463.7 jit_solution(7950284538344193213)
XLA Ops:
  6.5 0.0 all-gather.2.cloned.1.call-start
  6.5 0.7 all-gather.2.cloned.1.call-update
  7.3 32.2 %all-gather.2.cloned.1.call-done = bf16[192,8192]{1,0:T(8,128)(2,1)} async-done(((bf16[24,8192]{1,0:T(8,128)(2,1)}), bf16[192,8192]{1,0:T(8,128)(2,1)}) %all-gather.2.cloned.1.call-update) | async-done | bytes 3145744 | tf_op jit(solution)/shard_map/all_gather | solution.py:35
  39.5 3.9 copy.13
  43.4 0.0 copy-start.1
  43.4 0.0 copy-start.2
  43.4 0.0 copy-start.3
  43.4 6.9 %all-to-all-start = ((bf16[192,16,512]{2,0,1:T(8,128)(2,1)}), bf16[192,16,512]{2,0,1:T(8,128)(2,1)S(1)}, u32[]{:S(2)}, u32[]{:S(2)}) async-start(bf16[192,16,512]{2,0,1:T(8,128)(2,1)} %bitcast.15), calls=%async_computation | async-start | bytes 6291456 | tf_op jit(solution)/shard_map/all_to_all | solution.py:36
  50.3 0.0 reduce-scatter.6.cloned.1.call-start
  50.4 0.0 copy-done.1
  50.4 0.0 copy-done.2
  50.4 0.2 select_reduce_fusion.1
  50.6 0.0 copy-done.3
  50.6 0.2 select_reduce_fusion
  50.8 48.1 %all-to-all-done = bf16[192,16,512]{2,0,1:T(8,128)(2,1)S(1)} async-done(((bf16[192,16,512]{2,0,1:T(8,128)(2,1)}), bf16[192,16,512]{2,0,1:T(8,128)(2,1)S(1)}, u32[]{:S(2)}, u32[]{:S(2)}) %all-to-all-start) | async-done | bytes 3145760 | tf_op jit(solution)/shard_map/all_to_all | solution.py:36
  98.9 5.0 %gather_fusion = bf16[1024,512]{1,0:T(8,128)(2,1)} fusion(bf16[3072,512]{1,0:T(8,128)(2,1)S(1)} %bitcast.14, s32[1024]{0:T(1024)S(1)} %broadcast_clamp_fusion), kind=kCustom, calls=%fused_computation | custom fusion | bytes 2101248 | tf_op jit(solution)/shard_map/jit(_take)/gather | solution.py:37
  104.0 12.0 %fusion.1 = f32[1024,3696]{1,0:T(8,128)} fusion(bf16[512,3696]{0,1:T(8,128)(2,1)} %param.12, bf16[1024,512]{1,0:T(8,128)(2,1)} %gather_fusion, pred[1024]{0:T(1024)(128)(4,1)S(1)} %compare_and_fusion), kind=kOutput, calls=%fused_computation.8 | convolution fusion | flops 3876061184 | bytes 19973120 | tf_op jit(solution)/shard_map/dot_general | solution.py:47
  116.0 0.0 copy-start
  116.0 0.0 reduce-scatter.6.cloned.1.call-update
  116.0 0.0 reduce-scatter.4.cloned.1.call-start
  116.1 1.1 copy-done
  117.2 10.0 %fusion.2 = f32[1024,3696]{1,0:T(8,128)} fusion(bf16[512,3696]{0,1:T(8,128)(2,1)} %param.11, bf16[1024,512]{1,0:T(8,128)(2,1)S(1)} %copy-done, pred[1024]{0:T(1024)(128)(4,1)S(1)} %compare_and_fusion), kind=kOutput, calls=%fused_computation.9 | convolution fusion | flops 3876061184 | bytes 19973120 | tf_op jit(solution)/shard_map/dot_general | solution.py:40
  127.2 0.0 reduce-scatter.4.cloned.1.call-update
  127.2 0.0 reduce-scatter.8.cloned.1.call-start
  127.3 90.2 %reduce-scatter.6.cloned.1.call-done = f32[64,3696]{1,0:T(8,128)} async-done(((f32[1024,3696]{1,0:T(8,128)}), f32[64,3696]{1,0:T(8,128)}) %reduce-scatter.6.cloned.1.call-update) | async-done | bytes 946192 | tf_op jit(solution)/shard_map/reduce_scatter | solution.py:46
  217.5 106.4 %reduce-scatter.4.cloned.1.call-done = f32[64,3696]{1,0:T(8,128)} async-done(((f32[1024,3696]{1,0:T(8,128)}), f32[64,3696]{1,0:T(8,128)}) %reduce-scatter.4.cloned.1.call-update) | async-done | bytes 946192 | tf_op jit(solution)/shard_map/reduce_scatter | solution.py:39
  323.8 1.7 multiply_convert_fusion
  325.6 0.8 stack.2
  326.4 0.0 copy-start.4
  326.4 91.8 %all_to_all.24 = bf16[16,64,3696]{2,1,0:T(8,128)(2,1)S(1)} all-to-all(bf16[16,64,3696]{2,1,0:T(8,128)(2,1)S(1)} %stack.2), channel_id=1, replica_groups=mesh['row'=16,'col'=8] {'row'}, dimensions={0} | all-to-all | bytes 15138816 | tf_op jit(solution)/shard_map/all_to_all | solution.py:11
  418.2 0.0 copy-done.4
  418.2 5.6 %fusion.8 = f32[1024,512]{1,0:T(8,128)} fusion(bf16[1024,3696]{1,0:T(8,128)(2,1)S(1)} %bitcast.16, bf16[3696,512]{1,0:T(8,128)(2,1)S(1)} %copy-done.4), kind=kOutput, calls=%fused_computation.22 | convolution fusion | flops 3875536896 | bytes 13451264 | tf_op jit(solution)/shard_map/dot_general | solution.py:53
  423.8 0.0 reduce-scatter.8.cloned.1.call-update
  423.8 31.7 %reduce-scatter.8.cloned.1.call-done = f32[128,512]{1,0:T(8,128)} async-done(((f32[1024,512]{1,0:T(8,128)}), f32[128,512]{1,0:T(8,128)}) %reduce-scatter.8.cloned.1.call-update) | async-done | bytes 262160 | tf_op jit(solution)/shard_map/reduce_scatter | solution.py:56
  455.5 1.6 convert_element_type.7
  (4 shorter events, 0.0 us)
Async XLA Ops:
  6.5 32.9 %all-gather.2.cloned.1.call-start = ((), (), s32[]{:S(2)}) async-start(), calls=%async_computation.5 | async-start | bytes 3538944 | tf_op jit(solution)/shard_map/all_gather | solution.py:35
  43.4 7.0 %copy-start.1 = (s32[128]{0:T(128)S(1)}, s32[128]{0:T(128)}, u32[]{:S(2)}) copy-start(s32[128]{0:T(128)} %param.10) | copy-start | bytes 1540
  43.4 7.0 %copy-start.2 = (s32[128]{0:T(128)S(1)}, s32[128]{0:T(128)}, u32[]{:S(2)}) copy-start(s32[128]{0:T(128)} %param.8) | copy-start | bytes 1540
  43.4 7.2 %copy-start.3 = (s32[128]{0:T(128)S(1)}, s32[128]{0:T(128)}, u32[]{:S(2)}) copy-start(s32[128]{0:T(128)} %param.9) | copy-start | bytes 1540
  43.4 55.6 %all-to-all-start = ((bf16[192,16,512]{2,0,1:T(8,128)(2,1)}), bf16[192,16,512]{2,0,1:T(8,128)(2,1)S(1)}, u32[]{:S(2)}, u32[]{:S(2)}) async-start(bf16[192,16,512]{2,0,1:T(8,128)(2,1)} %bitcast.15), calls=%async_computation | async-start | bytes 6291456 | tf_op jit(solution)/shard_map/all_to_all | solution.py:36
  50.3 167.2 %reduce-scatter.6.cloned.1.call-start = ((), (), s32[]{:S(2)}) async-start(), calls=%async_computation.7 | async-start | bytes 16154624 | tf_op jit(solution)/shard_map/reduce_scatter | solution.py:46
  116.0 1.2 copy-start
  116.0 207.8 %reduce-scatter.4.cloned.1.call-start = ((), (), s32[]{:S(2)}) async-start(), calls=%async_computation.6 | async-start | bytes 16154624 | tf_op jit(solution)/shard_map/reduce_scatter | solution.py:39
  127.2 328.3 %reduce-scatter.8.cloned.1.call-start = ((), (), s32[]{:S(2)}) async-start(), calls=%async_computation.8 | async-start | bytes 2359296 | tf_op jit(solution)/shard_map/reduce_scatter | solution.py:56
  326.4 91.9 %copy-start.4 = (bf16[3696,512]{1,0:T(8,128)(2,1)S(1)}, bf16[3696,512]{1,0:T(8,128)(2,1)}, u32[]{:S(2)}) copy-start(bf16[3696,512]{1,0:T(8,128)(2,1)} %param.13) | copy-start | bytes 11354116
Sparse Core Ops, SparseCore 0:
  9.0 30.3 all-gather.1
  116.1 101.2 reduce-scatter.5
  220.9 102.8 reduce-scatter.3
  423.9 31.5 reduce-scatter.7
